TPU v7x, 256 devices: a whole 4x4x8 slice. The times are simulated.
256 devices in a mesh: dp: 32 (over x, z), seq: 8 (over y, core).
Axes of the slice: x: 4, y: 4, z: 8, core: 2. Of those that a mesh axis runs over, the one named last changes fastest.
Arguments:
- words: bfloat16 [128, 1024, 1024], P('dp', 'seq'), may hold values from -6 to 6
- patches: bfloat16 [128, 2048, 1024], P('dp', 'seq'), may hold values from -6 to 6
- proj: bfloat16 [1024, 1024], P('dp'), may hold values from -0.1875 to 0.1875
- routes: int32 [128, 1024, 1], P('dp', 'seq'), may hold values from 0 to 7; in each aligned block of 128 rows (0 to 127, 128 to 255, ..., all dimensions but the last counted through in order) at most 32 rows name the same one
- targets: int32 [128, 1024], P('dp', 'seq'), may hold values from 0 to 255
- counts: int32 [128], P('dp'), may hold values from 512 to 1024
- flags: int32 [128, 16, 32], P('dp'), may hold values 0 or 1
Outputs:
- word_loss: float32 [128, 1024], P('dp', 'seq')
- proj_grad: float32 [1024, 1024], P('dp', 'seq')
Inputs may be any that keep to these rules, and one draw needn't show every extreme that they name: `routes`: among the 128 words of one page held by one index of seq, at most 32 name the same shard; some block reaches 32.
All inputs are finite; a program needn't handle non-finite values. No bound on the sum of `flags` on one device may be relied on, other than what follows from the above.
Results may differ from a plain program's by a relative error of at most 0.0065.
Values may be sent and summed in bfloat16 or wider, within the bound.
A program may use at most 64 MiB of HBM per device.

v0:
```python
import math
import jax
import jax.numpy as jnp
from jax import lax
from jax.sharding import PartitionSpec as P

MARGIN_BLOCK_SIZE = 64


def local(words, patches, proj, routes, targets, counts, flags):
    pages, wdev, width = words.shape
    ppsz = patches.shape[1]
    nblk = flags.shape[1]
    nseq = lax.axis_size("seq")
    mine = lax.axis_index("seq")
    capacity_limit = 2 * wdev // nseq
    bps = ppsz // MARGIN_BLOCK_SIZE
    scale = 2.0 / math.sqrt(width)
    flat_rows = words.reshape(pages * wdev, width)
    columns = flat_rows
    query = jnp.dot(
        columns, lax.all_gather(proj, "dp", axis=0, tiled=True), preferred_element_type=jnp.float32
    )
    query = query.astype(jnp.bfloat16).reshape(pages, wdev, width)
    destination_slot = routes[:, :, 0]
    onehot = (
        destination_slot[:, :, None] == jnp.arange(nseq, dtype=jnp.int32)[None, None, :]
    ).astype(jnp.int32)
    rank = jnp.cumsum(onehot, axis=1) - onehot
    slot = jnp.sum(rank * onehot, axis=2)
    slot_hit = (
        slot[:, :, None] == jnp.arange(capacity_limit, dtype=jnp.int32)[None, None, :]
    ).astype(jnp.int32)
    dispatch = onehot[:, :, :, None] * slot_hit[:, :, None, :]
    dispatch_bf = dispatch.astype(jnp.bfloat16)
    word_idx = mine * wdev + jnp.arange(wdev, dtype=jnp.int32)
    q_buf = jnp.einsum(
        "pwhc,pwd->hpcd", dispatch_bf, query, preferred_element_type=jnp.float32
    ).astype(jnp.bfloat16)
    tgt_buf = jnp.einsum("pwhc,pw->hpc", dispatch, targets)
    idx_buf = jnp.einsum("pwhc,w->hpc", dispatch, word_idx + 1) - 1
    q_in, tgt_in, idx_in = (
        lax.all_to_all(q_buf, "seq", split_axis=0, concat_axis=0, tiled=True),
        lax.all_to_all(tgt_buf, "seq", split_axis=0, concat_axis=0, tiled=True),
        lax.all_to_all(idx_buf, "seq", split_axis=0, concat_axis=0, tiled=True),
    )
    scores = jnp.einsum("hpcd,pkd->hpck", q_in, patches, preferred_element_type=jnp.float32) * scale
    own = lax.dynamic_slice_in_dim(flags, mine * bps, bps, 2)
    word_block = jnp.maximum(idx_in, 0) // MARGIN_BLOCK_SIZE
    picked = (word_block[..., None] == jnp.arange(nblk, dtype=jnp.int32)).astype(jnp.int32)
    hit = jnp.sum(picked[..., None] * own[None, :, None, :, :], axis=-2)
    allowed = (hit > 0) | (
        (tgt_in // MARGIN_BLOCK_SIZE)[..., None] == jnp.arange(bps, dtype=jnp.int32)
    )
    mask = jnp.broadcast_to(allowed[..., None], allowed.shape + (MARGIN_BLOCK_SIZE,)).reshape(
        scores.shape
    )
    expo = jnp.where(mask, jnp.exp(scores), jnp.float32(0.0))
    total = jnp.sum(expo, axis=-1)
    is_target = jnp.arange(ppsz, dtype=jnp.int32) == tgt_in[..., None]
    target_score = jnp.sum(jnp.where(is_target, scores, jnp.float32(0.0)), axis=-1)
    valid_mask = (idx_in >= 0) & (idx_in < counts[None, :, None])
    loss_out = jnp.where(valid_mask, jnp.log(total) - target_score, jnp.float32(0.0))
    coef = jnp.where(
        valid_mask, jnp.float32(64.0) / counts.astype(jnp.float32)[None, :, None], jnp.float32(0.0)
    )
    dscore = (coef[..., None] * (expo / total[..., None] - is_target.astype(jnp.float32))).astype(
        jnp.bfloat16
    )
    dquery = (
        jnp.einsum("hpck,pkd->hpcd", dscore, patches, preferred_element_type=jnp.float32) * scale
    ).astype(jnp.bfloat16)
    loss_home = lax.all_to_all(loss_out, "seq", split_axis=0, concat_axis=0, tiled=True)
    dq_home = lax.all_to_all(dquery, "seq", split_axis=0, concat_axis=0, tiled=True)
    right = (
        jnp.einsum("pwhc,hpcd->pwd", dispatch_bf, dq_home, preferred_element_type=jnp.float32)
        .astype(jnp.bfloat16)
        .reshape(-1, width)
    )
    word_loss = jnp.einsum("pwhc,hpc->pw", dispatch.astype(jnp.float32), loss_home)
    columns = flat_rows
    partial_rows = lax.psum_scatter(
        jnp.einsum("rc,rd->cd", columns, right, preferred_element_type=jnp.float32),
        "dp",
        scatter_dimension=0,
        tiled=True,
    )
    proj_grad = lax.psum_scatter(partial_rows, "seq", scatter_dimension=1, tiled=True)
    return (word_loss, proj_grad)


def solution(mesh):
    in_specs = (
        P("dp", "seq", None),
        P("dp", "seq", None),
        P("dp", None),
        P("dp", "seq", None),
        P("dp", "seq"),
        P("dp"),
        P("dp", None, None),
    )
    out_specs = (P("dp", "seq"), P("dp", "seq"))
    return jax.shard_map(local, mesh=mesh, in_specs=in_specs, out_specs=out_specs, check_vma=False)
```

profile of v0, /device:TPU:4, one launch (start us, length us, event | category | flops | bytes accessed | tf_op | source)
XLA Modules:
  0.0 441.0 jit_solution(18329256724800153465)
XLA Ops:
  7.9 0.8 fusion.37
  9.1 0.9 select_reduce_fusion.1
  10.0 3.5 fusion.25
  14.2 4.5 %all-to-all-start = ((s32[8,1,128]{2,1,0:T(1,128)}), s32[8,1,128]{2,1,0:T(1,128)S(1)}, u32[]{:S(2)}, u32[]{:S(2)}) async-start(s32[8,1,128]{2,1,0:T(1,128)} %reshape.58), calls=%async_computation | async-start | bytes 8192 | tf_op jit(solution)/shard_map/all_to_all | solution.py:45
  18.7 4.2 fusion.23
  23.6 66.6 %all-gather.2.cloned.1.call-done = bf16[1024,1024]{1,0:T(8,128)(2,1)} async-done(((bf16[32,1024]{1,0:T(8,128)(2,1)}), bf16[1024,1024]{1,0:T(8,128)(2,1)}) %all-gather.2.cloned.1.call-update) | async-done | bytes 2097168 | tf_op jit(solution)/shard_map/all_gather | solution.py:22
  90.2 4.2 convolution_convert_fusion
  94.3 4.3 all-to-all-start.1
  98.6 3.3 convert_bitcast_fusion
  101.9 2.0 all-to-all-done.1
  103.9 4.4 all-to-all-start.2
  111.3 1.4 broadcast_in_dim.15
  113.5 21.9 %all-to-all-done.2 = bf16[8,4,32,1024]{3,2,1,0:T(8,128)(2,1)} async-done(((bf16[8,4,32,1024]{3,2,1,0:T(8,128)(2,1)}), bf16[8,4,32,1024]{3,2,1,0:T(8,128)(2,1)}, u32[]{:S(2)}, u32[]{:S(2)}) %all-to-all-start.2) | async-done | bytes 2097184 | tf_op jit(solution)/shard_map/all_to_all | solution.py:43
  135.4 2.7 fusion.27
  138.1 1.2 fusion.6
  139.3 30.8 %all_to_all.25 = bf16[8,4,32,1024]{3,2,1,0:T(8,128)(2,1)} all-to-all(bf16[8,4,32,1024]{3,2,1,0:T(8,128)(2,1)S(1)} %fusion.6), channel_id=1, replica_groups=mesh['dp'=32,'seq'=8] {'seq'}, dimensions={0} | all-to-all | bytes 4194304 | tf_op jit(solution)/shard_map/all_to_all | solution.py:74
  170.1 5.1 %convolution_bitcast_fusion = f32[1024,1024]{0,1:T(8,128)} fusion(bf16[4,128,1024]{2,1,0:T(8,128)(2,1)S(1)} %copy-done.1, bf16[8,4,32,1024]{3,2,1,0:T(8,128)(2,1)} %all_to_all.25, s32[4,128,32]{1,2,0:T(8,128)S(1)} %fusion.39, s32[4,128,8]{1,2,0:T(8,128)S(1)} %copy.34), kind=kOutput, calls=%fused_computation.1 | convolution fusion | flops 1342963712 | bytes 7421952 | tf_op jit(solution)/shard_map/rc,rd->cd/dot_general | solution.py:83
  175.2 5.3 %copy.63 = f32[1024,1024]{1,0:T(8,128)} copy(f32[1024,1024]{0,1:T(8,128)} %convolution_bitcast_fusion) | data formatting | bytes 8388608
  180.7 216.9 %reduce-scatter.7.cloned.1.call-done = f32[32,1024]{1,0:T(8,128)} async-done(((f32[1024,1024]{1,0:T(8,128)}), f32[32,1024]{1,0:T(8,128)}) %reduce-scatter.7.cloned.1.call-update) | async-done | bytes 131088
  397.6 1.9 copy.64
  399.5 9.4 %all_to_all.26 = bf16[8,4,32]{2,1,0:T(4,128)(2,1)S(1)} all-to-all(bf16[8,4,32]{2,1,0:T(4,128)(2,1)S(1)} %copy.49), channel_id=1, replica_groups=mesh['dp'=32,'seq'=8] {'seq'}, dimensions={0} | all-to-all | bytes 4096 | tf_op jit(solution)/shard_map/all_to_all | solution.py:73
  408.9 0.8 fusion.28
  409.7 23.2 %reduce-scatter.5.cloned.1.call-done = f32[32,128]{0,1:T(8,128)} async-done(((f32[32,1024]{0,1:T(8,128)}), f32[32,128]{0,1:T(8,128)}) %reduce-scatter.5.cloned.1.call-update) | async-done | bytes 16400 | tf_op jit(solution)/shard_map/reduce_scatter | solution.py:88
  432.9 1.5 copy.53
  (42 shorter events, 6.4 us)
Async XLA Ops:
  7.2 128.3 %copy-start = (bf16[4,256,1024]{2,1,0:T(8,128)(2,1)S(1)}, bf16[4,256,1024]{2,1,0:T(8,128)(2,1)}, u32[]{:S(2)}) copy-start(bf16[4,256,1024]{2,1,0:T(8,128)(2,1)} %param.8) | copy-start | bytes 6291460
  7.2 83.0 %all-gather.2.cloned.1.call-start = ((), (), s32[]{:S(2)}) async-start(), calls=%async_computation.7 | async-start | bytes 2162688 | tf_op jit(solution)/shard_map/all_gather | solution.py:22
  14.2 80.1 %all-to-all-start = ((s32[8,1,128]{2,1,0:T(1,128)}), s32[8,1,128]{2,1,0:T(1,128)S(1)}, u32[]{:S(2)}, u32[]{:S(2)}) async-start(s32[8,1,128]{2,1,0:T(1,128)} %reshape.58), calls=%async_computation | async-start | bytes 8192 | tf_op jit(solution)/shard_map/all_to_all | solution.py:45
  94.3 9.5 %all-to-all-start.1 = ((s32[8,1,128]{2,1,0:T(1,128)}), s32[8,1,128]{2,1,0:T(1,128)S(1)}, u32[]{:S(2)}, u32[]{:S(2)}) async-start(s32[8,1,128]{2,1,0:T(1,128)} %reshape.60), calls=%async_computation.1 | async-start | bytes 8192 | tf_op jit(solution)/shard_map/all_to_all | solution.py:44
  101.9 6.4 %copy-start.2 = (s32[4,16,32]{2,1,0:T(8,128)S(1)}, s32[4,16,32]{2,1,0:T(8,128)}, u32[]{:S(2)}) copy-start(s32[4,16,32]{2,1,0:T(8,128)} %param.13) | copy-start | bytes 24580
  101.9 6.6 %copy-start.3 = (s32[4]{0:T(128)S(1)}, s32[4]{0:T(128)}, u32[]{:S(2)}) copy-start(s32[4]{0:T(128)} %param.12) | copy-start | bytes 52
  103.9 31.6 %all-to-all-start.2 = ((bf16[8,4,32,1024]{3,2,1,0:T(8,128)(2,1)}), bf16[8,4,32,1024]{3,2,1,0:T(8,128)(2,1)}, u32[]{:S(2)}, u32[]{:S(2)}) async-start(bf16[8,4,32,1024]{3,2,1,0:T(8,128)(2,1)} %convert_bitcast_fusion), calls=%async_computation.2 | async-start | bytes 4194304 | tf_op jit(solution)/shard_map/all_to_all | solution.py:43
  108.2 289.3 %reduce-scatter.7.cloned.1.call-start = ((), (), s32[]{:S(2)}) async-start(), calls=%async_computation.9 | async-start | bytes 4325376
  139.3 30.8 %copy-start.1 = (bf16[4,128,1024]{2,1,0:T(8,128)(2,1)S(1)}, bf16[4,128,1024]{2,1,0:T(8,128)(2,1)}, u32[]{:S(2)}) copy-start(bf16[4,128,1024]{2,1,0:T(8,128)(2,1)} %param.7) | copy-start | bytes 3145732
  180.6 252.3 %reduce-scatter.5.cloned.1.call-start = ((), (), s32[]{:S(2)}) async-start(), calls=%async_computation.8 | async-start | bytes 589824 | tf_op jit(solution)/shard_map/reduce_scatter | solution.py:88
Sparse Core Ops, SparseCore 0:
  10.6 79.5 all-gather.1
  180.7 216.7 reduce-scatter.6
  400.2 32.6 reduce-scatter.4
where the time goes:
time: 442 us; the launch traced here: 441 us
  waiting for transfers between devices  331 us (75%)
  blocking collectives  40.2 us (9%)
  matrix products  24.9 us (6%)
  between operations  13.9 us (3%)
  local copies, waits for them, and re-layouts  13.6 us (3%)
  starting transfers between devices  13.3 us (3%)
    unnamed x4, waiting for transfers between devices  218 us
    all_gather x1, waiting for transfers between devices, local(): lax.all_gather(proj, 'dp', axis=0, tiled=True)  66.6 us
    all_to_all x1, blocking collectives, local(): lax.all_to_all(dquery, 'seq', split_axis=0, concat_axis=0, tiled=True)  30.8 us
    reduce_scatter x1, waiting for transfers between devices, local(): lax.psum_scatter(partial_rows, 'seq', scatter_dimension=1, tiled=True)  23.2 us
    all_to_all x1, waiting for transfers between devices, local(): lax.all_to_all(q_buf, 'seq', split_axis=0, concat_axis=0, tiled=True)  21.9 us
    unnamed x15, local copies, waits for them, and re-layouts  10.3 us
    all_to_all x1, blocking collectives, local(): lax.all_to_all(loss_out, 'seq', split_axis=0, concat_axis=0, tiled=True)  9.4 us
  transfers between devices with their start and end apart: 6, of which 5 were waited for; matrix products, arithmetic and copies ran while one was open for 6% of the time, Pallas kernels for 0%

commit v1 on v0

--- a/solution.py
+++ b/solution.py
@@ -19,7 +19,11 @@
     flat_rows = words.reshape(pages * wdev, width)
     columns = flat_rows
     query = jnp.dot(
-        columns, lax.all_gather(proj, "dp", axis=0, tiled=True), preferred_element_type=jnp.float32
+        columns,
+        jnp.concatenate(
+            lax.all_to_all(jnp.stack([proj] * lax.axis_size("dp")), "dp", 0, 0), axis=0
+        ),
+        preferred_element_type=jnp.float32,
     )
     query = query.astype(jnp.bfloat16).reshape(pages, wdev, width)
     destination_slot = routes[:, :, 0]

time: 442 us -> 427 us (0.966)
  waiting for transfers between devices: 331 us -> 304 us
  starting transfers between devices: 13.3 us -> 24.2 us
    all_gather x1 -> x0, waiting for transfers between devices: 66.6 us -> none  [local(): lax.all_gather(proj, 'dp', axis=0, tiled=True)]
    all_to_all x0 -> x1, waiting for transfers between devices: none -> 36.8 us  [local(): lax.all_to_all(jnp.stack([proj] * lax.axis_size('dp')), 'dp', 0, 0)]
    all_to_all x0 -> x1, starting transfers between devices: none -> 11.8 us  [local(): lax.all_to_all(jnp.stack([proj] * lax.axis_size('dp')), 'dp', 0, 0)]
    unnamed x4 -> x3, waiting for transfers between devices: 218 us -> 218 us
    unnamed x15 -> x21, local copies, waits for them, and re-layouts: 10.3 us -> 10.3 us
  transfers between devices with their start and end apart: 6 -> 6, of which waited for: 5 -> 6; matrix products, arithmetic and copies ran while one was open for 6% -> 6% of each run, Pallas kernels for 0% -> 0%
where the time goes in v1:
time: 427 us; the launch traced here: 426 us
  waiting for transfers between devices  304 us (71%)
  blocking collectives  40.1 us (9%)
  starting transfers between devices  24.2 us (6%)
  matrix products  23.8 us (6%)
  local copies, waits for them, and re-layouts  16.2 us (4%)
  between operations  14.2 us (3%)
    unnamed x3, waiting for transfers between devices  218 us
    all_to_all x1, waiting for transfers between devices, local(): lax.all_to_all(jnp.stack([proj] * lax.axis_size('dp')), 'dp', 0, 0)  36.8 us
    all_to_all x1, blocking collectives, local(): lax.all_to_all(dquery, 'seq', split_axis=0, concat_axis=0, tiled=True)  30.8 us
    reduce_scatter x1, waiting for transfers between devices, local(): lax.psum_scatter(partial_rows, 'seq', scatter_dimension=1, tiled=True)  23.2 us
    all_to_all x1, waiting for transfers between devices, local(): lax.all_to_all(q_buf, 'seq', split_axis=0, concat_axis=0, tiled=True)  21.9 us
    all_to_all x1, starting transfers between devices, local(): lax.all_to_all(jnp.stack([proj] * lax.axis_size('dp')), 'dp', 0, 0)  11.8 us
    unnamed x21, local copies, waits for them, and re-layouts  10.3 us
    all_to_all x1, blocking collectives, local(): lax.all_to_all(loss_out, 'seq', split_axis=0, concat_axis=0, tiled=True)  9.34 us
  transfers between devices with their start and end apart: 6, of which 6 were waited for; matrix products, arithmetic and copies ran while one was open for 6% of the time, Pallas kernels for 0%

profile of v1, /device:TPU:4, one launch (start us, length us, event | category | flops | bytes accessed | tf_op | source)
XLA Modules:
  0.0 426.3 jit_solution(423757124714431418)
XLA Ops:
  7.2 2.5 stack.2
  9.7 11.8 %all-to-all-start.2 = ((bf16[32,32,1024]{2,1,0:T(8,128)(2,1)}), bf16[32,32,1024]{2,1,0:T(8,128)(2,1)}, u32[]{:S(2)}, u32[]{:S(2)}) async-start(bf16[32,32,1024]{2,1,0:T(8,128)(2,1)} %stack.2), calls=%async_computation.2 | async-start | bytes 4194304 | tf_op jit(solution)/shard_map/all_to_all | solution.py:24
  23.9 3.5 fusion.25
  28.1 3.5 fusion.23
  32.3 36.8 %all-to-all-done.2 = bf16[32,32,1024]{2,1,0:T(8,128)(2,1)} async-done(((bf16[32,32,1024]{2,1,0:T(8,128)(2,1)}), bf16[32,32,1024]{2,1,0:T(8,128)(2,1)}, u32[]{:S(2)}, u32[]{:S(2)}) %all-to-all-start.2) | async-done | bytes 2097184 | tf_op jit(solution)/shard_map/all_to_all | solution.py:24
  69.1 4.5 %all-to-all-start = ((s32[8,1,128]{2,1,0:T(1,128)}), s32[8,1,128]{2,1,0:T(1,128)S(1)}, u32[]{:S(2)}, u32[]{:S(2)}) async-start(s32[8,1,128]{2,1,0:T(1,128)} %reshape.64), calls=%async_computation | async-start | bytes 8192 | tf_op jit(solution)/shard_map/all_to_all | solution.py:49
  73.6 3.8 convolution_convert_fusion
  77.4 1.4 all-to-all-done
  78.8 3.4 all-to-all-start.1
  82.2 3.3 convert_bitcast_fusion
  85.5 2.0 all-to-all-done.1
  87.5 4.4 %all-to-all-start.3 = ((bf16[8,4,32,1024]{3,2,1,0:T(8,128)(2,1)}), bf16[8,4,32,1024]{3,2,1,0:T(8,128)(2,1)}, u32[]{:S(2)}, u32[]{:S(2)}) async-start(bf16[8,4,32,1024]{3,2,1,0:T(8,128)(2,1)} %convert_bitcast_fusion), calls=%async_computation.3 | async-start | bytes 4194304 | tf_op jit(solution)/shard_map/all_to_all | solution.py:47
  94.9 1.4 broadcast_in_dim.15
  97.1 21.9 %all-to-all-done.3 = bf16[8,4,32,1024]{3,2,1,0:T(8,128)(2,1)} async-done(((bf16[8,4,32,1024]{3,2,1,0:T(8,128)(2,1)}), bf16[8,4,32,1024]{3,2,1,0:T(8,128)(2,1)}, u32[]{:S(2)}, u32[]{:S(2)}) %all-to-all-start.3) | async-done | bytes 2097184 | tf_op jit(solution)/shard_map/all_to_all | solution.py:47
  119.0 2.7 fusion.27
  121.7 1.2 fusion.6
  122.9 30.8 %all_to_all.30 = bf16[8,4,32,1024]{3,2,1,0:T(8,128)(2,1)} all-to-all(bf16[8,4,32,1024]{3,2,1,0:T(8,128)(2,1)S(1)} %fusion.6), channel_id=1, replica_groups=mesh['dp'=32,'seq'=8] {'seq'}, dimensions={0} | all-to-all | bytes 4194304 | tf_op jit(solution)/shard_map/all_to_all | solution.py:78
  153.7 5.1 %convolution_bitcast_fusion = f32[1024,1024]{0,1:T(8,128)} fusion(bf16[4,128,1024]{2,1,0:T(8,128)(2,1)S(1)} %copy-done.2, bf16[8,4,32,1024]{3,2,1,0:T(8,128)(2,1)} %all_to_all.30, s32[4,128,32]{1,2,0:T(8,128)S(1)} %fusion.39, s32[4,128,8]{1,2,0:T(8,128)S(1)} %copy.34), kind=kOutput, calls=%fused_computation.1 | convolution fusion | flops 1342963712 | bytes 7421952 | tf_op jit(solution)/shard_map/rc,rd->cd/dot_general | solution.py:87
  158.9 5.3 %copy.63 = f32[1024,1024]{1,0:T(8,128)} copy(f32[1024,1024]{0,1:T(8,128)} %convolution_bitcast_fusion) | data formatting | bytes 8388608
  164.3 218.4 %reduce-scatter.7.cloned.1.call-done = f32[32,1024]{1,0:T(8,128)} async-done(((f32[1024,1024]{1,0:T(8,128)}), f32[32,1024]{1,0:T(8,128)}) %reduce-scatter.7.cloned.1.call-update) | async-done | bytes 131088
  382.7 1.9 copy.64
  384.6 9.3 %all_to_all.31 = bf16[8,4,32]{2,1,0:T(4,128)(2,1)S(1)} all-to-all(bf16[8,4,32]{2,1,0:T(4,128)(2,1)S(1)} %copy.49), channel_id=1, replica_groups=mesh['dp'=32,'seq'=8] {'seq'}, dimensions={0} | all-to-all | bytes 4096 | tf_op jit(solution)/shard_map/all_to_all | solution.py:77
  394.8 23.2 %reduce-scatter.5.cloned.1.call-done = f32[32,128]{0,1:T(8,128)} async-done(((f32[32,1024]{0,1:T(8,128)}), f32[32,128]{0,1:T(8,128)}) %reduce-scatter.5.cloned.1.call-update) | async-done | bytes 16400 | tf_op jit(solution)/shard_map/reduce_scatter | solution.py:92
  418.0 1.5 copy.53
  (48 shorter events, 8.5 us)
Async XLA Ops:
  7.2 111.9 %copy-start = (bf16[4,256,1024]{2,1,0:T(8,128)(2,1)S(1)}, bf16[4,256,1024]{2,1,0:T(8,128)(2,1)}, u32[]{:S(2)}) copy-start(bf16[4,256,1024]{2,1,0:T(8,128)(2,1)} %param.8) | copy-start | bytes 6291460
  9.7 11.8 %copy-start.4 = (s32[4,128,1]{1,2,0:T(1,128)S(1)}, s32[4,128,1]{1,2,0:T(1,128)}, u32[]{:S(2)}) copy-start(s32[4,128,1]{1,2,0:T(1,128)} %param.10) | copy-start | bytes 6148
  9.7 18.4 %copy-start.6 = (s32[4,128]{1,0:T(4,128)S(1)}, s32[4,128]{1,0:T(4,128)}, u32[]{:S(2)}) copy-start(s32[4,128]{1,0:T(4,128)} %param.11) | copy-start | bytes 6148
  9.7 63.8 %copy-start.1 = (bf16[4,128,1024]{2,1,0:T(8,128)(2,1)S(1)}, bf16[4,128,1024]{2,1,0:T(8,128)(2,1)}, u32[]{:S(2)}) copy-start(bf16[4,128,1024]{2,1,0:T(8,128)(2,1)} %param.7) | copy-start | bytes 3145732
  9.7 59.4 %all-to-all-start.2 = ((bf16[32,32,1024]{2,1,0:T(8,128)(2,1)}), bf16[32,32,1024]{2,1,0:T(8,128)(2,1)}, u32[]{:S(2)}, u32[]{:S(2)}) async-start(bf16[32,32,1024]{2,1,0:T(8,128)(2,1)} %stack.2), calls=%async_computation.2 | async-start | bytes 4194304 | tf_op jit(solution)/shard_map/all_to_all | solution.py:24
  69.1 9.7 %all-to-all-start = ((s32[8,1,128]{2,1,0:T(1,128)}), s32[8,1,128]{2,1,0:T(1,128)S(1)}, u32[]{:S(2)}, u32[]{:S(2)}) async-start(s32[8,1,128]{2,1,0:T(1,128)} %reshape.64), calls=%async_computation | async-start | bytes 8192 | tf_op jit(solution)/shard_map/all_to_all | solution.py:49
  78.8 8.7 %all-to-all-start.1 = ((s32[8,1,128]{2,1,0:T(1,128)}), s32[8,1,128]{2,1,0:T(1,128)S(1)}, u32[]{:S(2)}, u32[]{:S(2)}) async-start(s32[8,1,128]{2,1,0:T(1,128)} %reshape.66), calls=%async_computation.1 | async-start | bytes 8192 | tf_op jit(solution)/shard_map/all_to_all | solution.py:48
  85.5 6.4 %copy-start.3 = (s32[4,16,32]{2,1,0:T(8,128)S(1)}, s32[4,16,32]{2,1,0:T(8,128)}, u32[]{:S(2)}) copy-start(s32[4,16,32]{2,1,0:T(8,128)} %param.13) | copy-start | bytes 24580
  85.5 6.6 %copy-start.5 = (s32[4]{0:T(128)S(1)}, s32[4]{0:T(128)}, u32[]{:S(2)}) copy-start(s32[4]{0:T(128)} %param.12) | copy-start | bytes 52
  87.5 31.6 %all-to-all-start.3 = ((bf16[8,4,32,1024]{3,2,1,0:T(8,128)(2,1)}), bf16[8,4,32,1024]{3,2,1,0:T(8,128)(2,1)}, u32[]{:S(2)}, u32[]{:S(2)}) async-start(bf16[8,4,32,1024]{3,2,1,0:T(8,128)(2,1)} %convert_bitcast_fusion), calls=%async_computation.3 | async-start | bytes 4194304 | tf_op jit(solution)/shard_map/all_to_all | solution.py:47
  91.8 290.8 %reduce-scatter.7.cloned.1.call-start = ((), (), s32[]{:S(2)}) async-start(), calls=%async_computation.9 | async-start | bytes 4325376
  122.9 30.8 %copy-start.2 = (bf16[4,128,1024]{2,1,0:T(8,128)(2,1)S(1)}, bf16[4,128,1024]{2,1,0:T(8,128)(2,1)}, u32[]{:S(2)}) copy-start(bf16[4,128,1024]{2,1,0:T(8,128)(2,1)} %param.7) | copy-start | bytes 3145732
  164.2 253.7 %reduce-scatter.5.cloned.1.call-start = ((), (), s32[]{:S(2)}) async-start(), calls=%async_computation.8 | async-start | bytes 589824 | tf_op jit(solution)/shard_map/reduce_scatter | solution.py:92
Sparse Core Ops, SparseCore 0:
  164.3 218.2 reduce-scatter.6
  385.3 32.5 reduce-scatter.4
